TPU v7x, 32 devices: a whole 2x2x4 slice. The times are simulated.
32 devices in a mesh: gx: 8 (over z, x), gy: 4 (over y, core).
Axes of the slice: x: 2, y: 2, z: 4, core: 2. Of those that a mesh axis runs over, the one named last changes fastest.
Arguments:
- right_side: float32 [4096, 128], P(('gx', 'gy'))
- compress: float32 [4096, 128], P(('gx', 'gy')), may hold values from 0.5 to 8
- block_fill: int32 [4096], P(('gx', 'gy')), may hold values from 32 to 128, as said below
- pair_home: int32 [12288], P(('gx', 'gy')), may hold values from 0 to 4095, as said below
- pair_far: int32 [12288], P(('gx', 'gy')), may hold values from 0 to 4095, as said below
- pair_count: int32 [32], P(('gx', 'gy')), may hold values from 1 to 384, as said below
- weights: bfloat16 [12288, 128, 128], P(('gx', 'gy')), may hold values from 0 to 0.015625
Outputs:
- solution_field: float32 [4096, 128], P(('gx', 'gy'))
- residual: float32 [4096, 128], P(('gx', 'gy'))
Inputs may be any that keep to these rules, and one draw needn't show every extreme that they name: `pair_home`: pair slot s names as first block a block of device s // 384, blocks of device d being d * 128 to d * 128 + 127, devices numbered gx major. `pair_far`: the second block belongs to the slot's device or to one of its eight neighbours on the periodic gx by gy grid of devices. `pair_count`: slots after a device's count are ignored; some devices hold 384. `block_fill`: slots after a block's fill are padding; some block holds 128.
All inputs are finite; a program needn't handle non-finite values.
Results may differ from a plain program's by a relative error of at most 0.015.
Values may be sent and summed in bfloat16 or wider, within the bound.
A program may use at most 64 MiB of HBM per device.

v0:
```python
import math
import jax
import jax.numpy as jnp
from jax import lax
from jax.sharding import PartitionSpec as P

ITERS = 3


def extended(block, sides, width):
    for axis, dim in sides:
        count = lax.axis_size(axis)
        forward = [(i, i + 1) for i in range(count - 1)]
        forward.append((count - 1, 0))
        backward = [(target, source) for source, target in forward]
        low = lax.ppermute(
            lax.slice_in_dim(block, block.shape[dim] - width, None, axis=dim), axis, forward
        )
        high = lax.ppermute(lax.slice_in_dim(block, 0, width, axis=dim), axis, backward)
        block = jnp.concatenate([low, block, high], axis=dim)
    return block


def passed_along(value, axis, steps):
    count = lax.axis_size(axis)
    pairs = [(source, (source + steps) % count) for source in range(count)]
    return lax.ppermute(value, axis, pairs)


def neighbours(quant):
    return extended(quant[None, None], (("gx", 0), ("gy", 1)), 1)


def return_terms(far_totals, blocks, tile_size):
    parts = far_totals.reshape(3, 3, blocks, tile_size)
    column = parts[1]
    for offset, slab in ((1, parts[2]), (-1, parts[0])):
        column = column + passed_along(slab.astype(jnp.bfloat16), "gx", offset).astype(slab.dtype)
    total = column[1]
    for offset, slab in ((1, column[2]), (-1, column[0])):
        total = total + passed_along(slab.astype(jnp.bfloat16), "gy", offset).astype(slab.dtype)
    return total


def on_device(right_side, compress, block_fill, pair_home, pair_far, pair_count, weights):
    blocks, tile_size = right_side.shape
    npairs = weights.shape[0]
    size_second = lax.axis_size("gy")
    size_first = lax.axis_size("gx")
    first_index = lax.axis_index("gx")
    second_index = lax.axis_index("gy")
    my_device = first_index * size_second + second_index
    live = (jnp.arange(tile_size, dtype=jnp.int32)[None, :] < block_fill[:, None]).astype(
        jnp.float32
    )
    home_local = pair_home - my_device * blocks
    far_device = pair_far // blocks
    far_inside = pair_far % blocks
    slot_first = (far_device // size_second - first_index + 1) % size_first
    slot_second = (far_device % size_second - second_index + 1) % size_second
    far_slot = (slot_first * 3 + slot_second) * blocks + far_inside
    row_sum = jnp.sum(weights, axis=2, dtype=jnp.float32)
    col_sum = jnp.sum(weights, axis=1, dtype=jnp.float32)
    count = pair_count[0]
    group = math.gcd(npairs, 32)
    rounds = (count + group - 1) // group

    def operate(field):
        quant = (live * field).astype(jnp.bfloat16)
        nearby = neighbours(quant).reshape(9 * blocks, tile_size)

        def one_group(group_id, totals):
            home_totals, far_totals = totals
            start = group_id * group
            tiles = lax.dynamic_slice_in_dim(weights, start, group, 0)
            homes = lax.dynamic_slice_in_dim(home_local, start, group, 0)
            slots = lax.dynamic_slice_in_dim(far_slot, start, group, 0)
            rows_part = lax.dynamic_slice_in_dim(row_sum, start, group, 0)
            cols_part = lax.dynamic_slice_in_dim(col_sum, start, group, 0)
            first = quant[homes]
            second = nearby[slots]
            toward = jnp.einsum("pij,pj->pi", tiles, second, preferred_element_type=jnp.float32)
            backward = jnp.einsum("pij,pi->pj", tiles, first, preferred_element_type=jnp.float32)
            keep = (start + jnp.arange(group, dtype=jnp.int32) < count).astype(jnp.float32)[:, None]
            term_home = (rows_part * first.astype(jnp.float32) - toward) * keep
            term_far = (cols_part * second.astype(jnp.float32) - backward) * keep
            return (home_totals.at[homes].add(term_home), far_totals.at[slots].add(term_far))

        start_totals = (
            jnp.zeros((blocks, tile_size), jnp.float32),
            jnp.zeros((9 * blocks, tile_size), jnp.float32),
        )
        home_totals, far_totals = lax.fori_loop(0, rounds, one_group, start_totals)
        pairs_sum = home_totals + return_terms(far_totals, blocks, tile_size)
        return compress * field + live * pairs_sum

    def two_products(vector, image):
        return lax.psum((jnp.sum(vector * vector), jnp.sum(vector * image)), ("gx", "gy"))

    solution_field = jnp.zeros_like(right_side)
    residual = right_side
    image = operate(residual)
    norm_now, product = two_products(residual, image)
    alpha = norm_now / product
    direction, along = (residual, image)
    for step in range(ITERS):
        solution_field = solution_field + alpha * direction
        residual = residual - alpha * along
        if step + 1 < ITERS:
            image = operate(residual)
            norm_next, product = two_products(residual, image)
            ratio = norm_next / norm_now
            alpha = norm_next / (product - ratio * norm_next / alpha)
            direction = residual + ratio * direction
            along = image + ratio * along
            norm_now = norm_next
    return (solution_field, residual)


def solution(mesh):
    return jax.shard_map(
        on_device,
        mesh=mesh,
        in_specs=(
            P(("gx", "gy"), None),
            P(("gx", "gy"), None),
            P(("gx", "gy")),
            P(("gx", "gy")),
            P(("gx", "gy")),
            P(("gx", "gy")),
            P(("gx", "gy"), None, None),
        ),
        out_specs=(P(("gx", "gy"), None), P(("gx", "gy"), None)),
        check_vma=False,
    )
```

profile of v0, /device:TPU:12, one launch (start us, length us, event | category | flops | bytes accessed | tf_op | source)
XLA Modules:
  0.0 470.0 jit_solution(12141780659297116652)
XLA Ops:
  3.7 7.8 %convert_reduce_fusion = (f32[384,128]{1,0:T(8,128)S(1)}, f32[384,128]{1,0:T(8,128)S(1)}) fusion(bf16[384,128,128]{2,1,0:T(8,128)(2,1)} %param.19), kind=kLoop, calls=%fused_computation.93 | loop fusion | flops 18776064 | bytes 12976128 | tf_op jit(solution)/shard_map/reduce_sum | solution.py:63
  16.4 29.4 %while.36 = (s32[]{:T(128)}, f32[128,128]{1,0:T(8,128)S(1)}, f32[1152,128]{1,0:T(8,128)S(1)}, s32[]{:T(128)}, s32[384]{0:T(512)S(1)}, /*index=5*/f32[384,128]{1,...) while((s32[]{:T(128)}, f32[128,128]{1,0:T(8,128)S(1)}, ...), condition=%wide.region_7.8_spmd, body=%wide.region_4.7_spmd.sunk | while | flops 2140454 | bytes 2926959 | solution.py:93
  17.1 1.8 fusion.132
  24.5 1.8 fusion.132
  31.8 1.8 fusion.132
  39.2 1.8 fusion.132
  45.9 2.0 collective-permute-start.4
  48.0 3.9 collective-permute-done.5
  57.8 100.2 %all-reduce.2 = (f32[]{:T(128)}, f32[]{:T(128)}) all-reduce(f32[]{:T(128)} %get-tuple-element.207, f32[]{:T(128)} %get-tuple-element.206), channel_id=1, replica_groups=mesh['gx'=8,'gy'=4] {'gx','gy'}, use_global_device_ids=true, to_apply=%region_1.2 | all-reduce | flops 2 | bytes 16 | tf_op jit(solution)/shard_map/psum | solution.py:98
  161.5 1.9 collective-permute-done.9
  163.4 2.1 collective-permute-done.8
  166.0 2.5 collective-permute-done.11
  169.9 29.4 %while.37 = (s32[]{:T(128)}, f32[128,128]{1,0:T(8,128)S(1)}, f32[1152,128]{1,0:T(8,128)S(1)}, s32[]{:T(128)}, s32[384]{0:T(512)S(1)}, /*index=5*/f32[384,128]{1,...) while((s32[]{:T(128)}, f32[128,128]{1,0:T(8,128)S(1)}, ...), condition=%wide.region_15.16_spmd, body=%wide.region_12.15_spmd.sunk | while | flops 2140454 | bytes 2926959 | solution.py:93
  170.6 1.8 fusion.140
  178.0 1.8 fusion.140
  185.3 1.8 fusion.140
  192.7 1.8 fusion.140
  199.5 2.0 collective-permute-start.12
  201.5 3.0 collective-permute-done.13
  204.5 3.1 collective-permute-done.12
  211.9 98.5 %all-reduce.1 = (f32[]{:T(128)}, f32[]{:T(128)}) all-reduce(f32[]{:T(128)} %get-tuple-element.205, f32[]{:T(128)} %get-tuple-element.204), channel_id=1, replica_groups=mesh['gx'=8,'gy'=4] {'gx','gy'}, use_global_device_ids=true, to_apply=%region_11.12 | all-reduce | flops 2 | bytes 16 | tf_op jit(solution)/shard_map/psum | solution.py:98
  316.8 1.9 collective-permute-done.17
  320.7 2.6 collective-permute-done.19
  324.6 29.4 %while.38 = (s32[]{:T(128)}, f32[128,128]{1,0:T(8,128)S(1)}, f32[1152,128]{1,0:T(8,128)S(1)}, s32[]{:T(128)}, s32[384]{0:T(512)S(1)}, /*index=5*/f32[384,128]{1,...) while((s32[]{:T(128)}, f32[128,128]{1,0:T(8,128)S(1)}, ...), condition=%wide.region_23.24_spmd, body=%wide.region_20.23_spmd.sunk | while | flops 2140454 | bytes 2926959 | solution.py:93
  325.3 1.8 fusion.148
  332.6 1.8 fusion.148
  340.0 1.8 fusion.148
  347.3 1.8 fusion.148
  354.1 2.0 collective-permute-start.20
  356.1 2.9 collective-permute-done.21
  359.0 3.2 collective-permute-done.20
  366.4 99.1 %all-reduce = (f32[]{:T(128)}, f32[]{:T(128)}) all-reduce(f32[]{:T(128)} %get-tuple-element.203, f32[]{:T(128)} %get-tuple-element.202), channel_id=1, replica_groups=mesh['gx'=8,'gy'=4] {'gx','gy'}, use_global_device_ids=true, to_apply=%region_19.20 | all-reduce | flops 2 | bytes 16 | tf_op jit(solution)/shard_map/psum | solution.py:98
  (189 shorter events, 97.5 us)
Async XLA Ops:
  0.6 10.9 %copy-start.2 = (s32[128]{0:T(128)S(1)}, s32[128]{0:T(128)}, u32[]{:S(2)}) copy-start(s32[128]{0:T(128)} %param.15) | copy-start | bytes 1540
  0.6 10.9 %copy-start = (f32[128,128]{1,0:T(8,128)S(1)}, f32[128,128]{1,0:T(8,128)}, u32[]{:S(2)}) copy-start(f32[128,128]{1,0:T(8,128)} %param.13) | copy-start | bytes 196612
  0.7 11.6 %copy-start.3 = (s32[384]{0:T(512)S(1)}, s32[384]{0:T(512)}, u32[]{:S(2)}) copy-start(s32[384]{0:T(512)} %param.17) | copy-start | bytes 4612
  0.7 11.6 %copy-start.4 = (s32[384]{0:T(512)S(1)}, s32[384]{0:T(512)}, u32[]{:S(2)}) copy-start(s32[384]{0:T(512)} %param.16) | copy-start | bytes 4612
  1.6 10.0 %collective-permute-start.1 = (bf16[1,1,128,128]{3,2,1,0:T(8,128)(2,1)S(1)}, bf16[1,1,128,128]{3,2,1,0:T(8,128)(2,1)S(1)}, u32[]{:S(2)}, u32[]{:S(2)}) collective-permute-start(bf16[1,1,128,128]{3,2,1,0:T(8,128)(2,1)S(1)} %fusion.101), channel_id=1, source_target_pairs={{4,0},{8,4},{12,8},{16,12},{20,16},{24,20},{28,24},{0,28},{5,1},{9... | collective-permute-start | bytes 98312 | tf_op jit(solution)/shard_map/ppermute | solution.py:19
  3.1 8.6 %collective-permute-start = (bf16[1,1,128,128]{3,2,1,0:T(8,128)(2,1)S(1)}, bf16[1,1,128,128]{3,2,1,0:T(8,128)(2,1)S(1)}, u32[]{:S(2)}, u32[]{:S(2)}) collective-permute-start(bf16[1,1,128,128]{3,2,1,0:T(8,128)(2,1)S(1)} %fusion.101), channel_id=1, source_target_pairs={{0,4},{4,8},{8,12},{12,16},{16,20},{20,24},{24,28},{28,0},{1,5},{5... | collective-permute-start | bytes 98312 | tf_op jit(solution)/shard_map/ppermute | solution.py:16
  11.5 45.5 %copy-start.1 = (f32[128,128]{1,0:T(8,128)S(1)}, f32[128,128]{1,0:T(8,128)}, u32[]{:S(2)}) copy-start(f32[128,128]{1,0:T(8,128)} %param.14) | copy-start | bytes 196612
  11.7 2.9 collective-permute-start.3
  11.8 4.5 collective-permute-start.2
  45.9 6.0 %collective-permute-start.5 = (bf16[3,128,128]{2,1,0:T(8,128)(2,1)S(1)}, bf16[3,128,128]{2,1,0:T(8,128)(2,1)S(1)}, u32[]{:S(2)}, u32[]{:S(2)}) collective-permute-start(bf16[3,128,128]{2,1,0:T(8,128)(2,1)S(1)} %bitcast.143), channel_id=1, source_target_pairs={{0,28},{4,0},{8,4},{12,8},{16,12},{20,16},{24,20},{28,24},{1,29},{... | collective-permute-start | bytes 294920 | tf_op jit(solution)/shard_map/ppermute | solution.py:27
  45.9 7.3 %collective-permute-start.4 = (bf16[3,128,128]{2,1,0:T(8,128)(2,1)S(1)}, bf16[3,128,128]{2,1,0:T(8,128)(2,1)S(1)}, u32[]{:S(2)}, u32[]{:S(2)}) collective-permute-start(bf16[3,128,128]{2,1,0:T(8,128)(2,1)S(1)} %bitcast.140), channel_id=1, source_target_pairs={{0,4},{4,8},{8,12},{12,16},{16,20},{20,24},{24,28},{28,0},{1,5},{5... | collective-permute-start | bytes 294920 | tf_op jit(solution)/shard_map/ppermute | solution.py:27
  53.3 2.0 collective-permute-start.7
  53.7 3.3 collective-permute-start.6
  159.4 4.0 collective-permute-start.9
  160.6 4.8 %collective-permute-start.8 = (bf16[1,1,128,128]{3,2,1,0:T(8,128)(2,1)S(1)}, bf16[1,1,128,128]{3,2,1,0:T(8,128)(2,1)S(1)}, u32[]{:S(2)}, u32[]{:S(2)}) collective-permute-start(bf16[1,1,128,128]{3,2,1,0:T(8,128)(2,1)S(1)} %bitcast.119), channel_id=1, source_target_pairs={{0,4},{4,8},{8,12},{12,16},{16,20},{20,24},{24,28},{28,0},{1,5},{5... | collective-permute-start | bytes 98312 | tf_op jit(solution)/shard_map/ppermute | solution.py:16
  165.5 3.1 collective-permute-start.11
  165.5 4.3 collective-permute-start.10
  199.4 5.1 %collective-permute-start.13 = (bf16[3,128,128]{2,1,0:T(8,128)(2,1)S(1)}, bf16[3,128,128]{2,1,0:T(8,128)(2,1)S(1)}, u32[]{:S(2)}, u32[]{:S(2)}) collective-permute-start(bf16[3,128,128]{2,1,0:T(8,128)(2,1)S(1)} %bitcast.144), channel_id=1, source_target_pairs={{0,28},{4,0},{8,4},{12,8},{16,12},{20,16},{24,20},{28,24},{1,29},{... | collective-permute-start | bytes 294920 | tf_op jit(solution)/shard_map/ppermute | solution.py:27
  199.5 8.1 %collective-permute-start.12 = (bf16[3,128,128]{2,1,0:T(8,128)(2,1)S(1)}, bf16[3,128,128]{2,1,0:T(8,128)(2,1)S(1)}, u32[]{:S(2)}, u32[]{:S(2)}) collective-permute-start(bf16[3,128,128]{2,1,0:T(8,128)(2,1)S(1)} %bitcast.141), channel_id=1, source_target_pairs={{0,4},{4,8},{8,12},{12,16},{16,20},{20,24},{24,28},{28,0},{1,5},{5... | collective-permute-start | bytes 294920 | tf_op jit(solution)/shard_map/ppermute | solution.py:27
  207.6 1.7 collective-permute-start.15
  207.7 3.4 collective-permute-start.14
  314.8 4.0 collective-permute-start.17
  315.3 4.8 %collective-permute-start.16 = (bf16[1,1,128,128]{3,2,1,0:T(8,128)(2,1)S(1)}, bf16[1,1,128,128]{3,2,1,0:T(8,128)(2,1)S(1)}, u32[]{:S(2)}, u32[]{:S(2)}) collective-permute-start(bf16[1,1,128,128]{3,2,1,0:T(8,128)(2,1)S(1)} %bitcast.115), channel_id=1, source_target_pairs={{0,4},{4,8},{8,12},{12,16},{16,20},{20,24},{24,28},{28,0},{1,5},{5... | collective-permute-start | bytes 98312 | tf_op jit(solution)/shard_map/ppermute | solution.py:16
  320.2 3.2 collective-permute-start.19
  320.2 4.2 collective-permute-start.18
  354.0 5.0 %collective-permute-start.21 = (bf16[3,128,128]{2,1,0:T(8,128)(2,1)S(1)}, bf16[3,128,128]{2,1,0:T(8,128)(2,1)S(1)}, u32[]{:S(2)}, u32[]{:S(2)}) collective-permute-start(bf16[3,128,128]{2,1,0:T(8,128)(2,1)S(1)} %bitcast.145), channel_id=1, source_target_pairs={{0,28},{4,0},{8,4},{12,8},{16,12},{20,16},{24,20},{28,24},{1,29},{... | collective-permute-start | bytes 294920 | tf_op jit(solution)/shard_map/ppermute | solution.py:27
  354.1 8.1 %collective-permute-start.20 = (bf16[3,128,128]{2,1,0:T(8,128)(2,1)S(1)}, bf16[3,128,128]{2,1,0:T(8,128)(2,1)S(1)}, u32[]{:S(2)}, u32[]{:S(2)}) collective-permute-start(bf16[3,128,128]{2,1,0:T(8,128)(2,1)S(1)} %bitcast.142), channel_id=1, source_target_pairs={{0,4},{4,8},{8,12},{12,16},{16,20},{20,24},{24,28},{28,0},{1,5},{5... | collective-permute-start | bytes 294920 | tf_op jit(solution)/shard_map/ppermute | solution.py:27
  362.3 1.7 collective-permute-start.23
  362.4 3.4 collective-permute-start.22
where the time goes:
time: 474 us; the launch traced here: 470 us
  blocking collectives  298 us (63%)
  waiting for transfers between devices  44.5 us (9%)
  other arithmetic  43.9 us (9%)
  matrix products  41.4 us (9%)
  starting transfers between devices  15.8 us (3%)
  local copies, waits for them, and re-layouts  14.9 us (3%)
  between operations  11.1 us (2%)
    psum x3, blocking collectives, two_products(): lax.psum((jnp.sum(vector * vector), jnp.sum(vector * image)), ('gx', 'gy'))  298 us
    ppermute x12, waiting for transfers between devices, passed_along(): return lax.ppermute(value, axis, pairs)  26.4 us
    dot_general x12, matrix products, one_group(): jnp.einsum('pij,pj->pi', tiles, second, preferred_element_type=jnp.float32)  22.2 us
    dot_general x12, matrix products, one_group(): jnp.einsum('pij,pi->pj', tiles, first, preferred_element_type=jnp.float32)  19.2 us
    scatter-add x12, other arithmetic, one_group(): far_totals.at[slots].add(term_far)  12.5 us
    ppermute x6, waiting for transfers between devices, extended(): lax.ppermute(lax.slice_in_dim(block, 0, width, axis=dim), axis, backward)  10.6 us
    scatter-add x12, other arithmetic, one_group(): home_totals.at[homes].add(term_home)  10.3 us
  transfers between devices with their start and end apart: 24, of which 22 were waited for; matrix products, arithmetic and copies ran while one was open for 2% of the time, Pallas kernels for 0%

commit v1 on v0

--- a/solution.py
+++ b/solution.py
@@ -95,7 +95,7 @@
         return compress * field + live * pairs_sum
 
     def two_products(vector, image):
-        return lax.psum((jnp.sum(vector * vector), jnp.sum(vector * image)), ("gx", "gy"))
+        return lax.psum(lax.psum((jnp.sum(vector * vector), jnp.sum(vector * image)), "gy"), "gx")
 
     solution_field = jnp.zeros_like(right_side)
     residual = right_side

time: 474 us -> 424 us (0.89)
  the two profiles are of different devices: /device:TPU:12 before, /device:TPU:0 now
where the time goes in v1:
time: 424 us; the launch traced here: 420 us
  waiting for transfers between devices  229 us (54%)
  blocking collectives  78.9 us (19%)
  other arithmetic  36.1 us (9%)
  matrix products  31.1 us (7%)
  starting transfers between devices  22.6 us (5%)
  between operations  11.3 us (3%)
  local copies, waits for them, and re-layouts  11.2 us (3%)
    ppermute x12, waiting for transfers between devices, passed_along(): return lax.ppermute(value, axis, pairs)  207 us
    psum x3, blocking collectives, two_products(): lax.psum(lax.psum((jnp.sum(vector * vector), jnp.sum(vector * image)), 'g...  59.4 us
    psum x3, blocking collectives, two_products(): lax.psum((jnp.sum(vector * vector), jnp.sum(vector * image)), 'gy')  19.5 us
    dot_general x9, matrix products, one_group(): jnp.einsum('pij,pj->pi', tiles, second, preferred_element_type=jnp.float32)  16.6 us
    dot_general x9, matrix products, one_group(): jnp.einsum('pij,pi->pj', tiles, first, preferred_element_type=jnp.float32)  14.4 us
    ppermute x6, waiting for transfers between devices, extended(): lax.ppermute(lax.slice_in_dim(block, block.shape[dim] - width, None, axis...  11.3 us
    ppermute x12, starting transfers between devices, passed_along(): return lax.ppermute(value, axis, pairs)  10.6 us
    ppermute x6, waiting for transfers between devices, extended(): lax.ppermute(lax.slice_in_dim(block, 0, width, axis=dim), axis, backward)  10.3 us
  transfers between devices with their start and end apart: 24, of which 22 were waited for; matrix products, arithmetic and copies ran while one was open for 2% of the time, Pallas kernels for 0%

profile of v1, /device:TPU:0, one launch (start us, length us, event | category | flops | bytes accessed | tf_op | source)
XLA Modules:
  0.0 420.4 jit_solution(13583172684030943972)
XLA Ops:
  1.6 6.1 %collective-permute-start.1 = (bf16[1,1,128,128]{3,2,1,0:T(8,128)(2,1)S(1)}, bf16[1,1,128,128]{3,2,1,0:T(8,128)(2,1)S(1)}, u32[]{:S(2)}, u32[]{:S(2)}) collective-permute-start(bf16[1,1,128,128]{3,2,1,0:T(8,128)(2,1)S(1)} %fusion.101), channel_id=1, source_target_pairs={{4,0},{8,4},{12,8},{16,12},{20,16},{24,20},{28,24},{0,28},{5,1},{9... | collective-permute-start | bytes 98312 | tf_op jit(solution)/shard_map/ppermute | solution.py:19
  7.7 7.8 %convert_reduce_fusion = (f32[384,128]{1,0:T(8,128)S(1)}, f32[384,128]{1,0:T(8,128)S(1)}) fusion(bf16[384,128,128]{2,1,0:T(8,128)(2,1)} %param.19), kind=kLoop, calls=%fused_computation.93 | loop fusion | flops 18776064 | bytes 12976128 | tf_op jit(solution)/shard_map/reduce_sum | solution.py:63
  17.1 2.1 collective-permute-done.3
  21.0 22.1 %while.36 = (s32[]{:T(128)}, f32[128,128]{1,0:T(8,128)S(1)}, f32[1152,128]{1,0:T(8,128)S(1)}, s32[]{:T(128)}, s32[384]{0:T(512)S(1)}, /*index=5*/f32[384,128]{1,...) while((s32[]{:T(128)}, f32[128,128]{1,0:T(8,128)S(1)}, ...), condition=%wide.region_8.9_spmd, body=%wide.region_5.8_spmd.sunk | while | flops 2140454 | bytes 2926959 | solution.py:93
  21.7 1.8 fusion.132
  29.1 1.8 fusion.132
  43.1 4.8 %collective-permute-start.5 = (bf16[3,128,128]{2,1,0:T(8,128)(2,1)S(1)}, bf16[3,128,128]{2,1,0:T(8,128)(2,1)S(1)}, u32[]{:S(2)}, u32[]{:S(2)}) collective-permute-start(bf16[3,128,128]{2,1,0:T(8,128)(2,1)S(1)} %bitcast.143), channel_id=1, source_target_pairs={{0,28},{4,0},{8,4},{12,8},{16,12},{20,16},{24,20},{28,24},{1,29},{... | collective-permute-start | bytes 294920 | tf_op jit(solution)/shard_map/ppermute | solution.py:27
  47.9 2.2 collective-permute-done.5
  50.1 64.4 %collective-permute-done.4 = bf16[3,128,128]{2,1,0:T(8,128)(2,1)S(1)} collective-permute-done((bf16[3,128,128]{2,1,0:T(8,128)(2,1)S(1)}, bf16[3,128,128]{2,1,0:T(8,128)(2,1)S(1)}, u32[]{:S(2)}, u32[]{:S(2)}) %collective-permute-start.4) | collective-permute-done | bytes 98336 | tf_op jit(solution)/shard_map/ppermute | solution.py:27
  118.8 6.3 %all-reduce.5 = (f32[]{:T(128)}, f32[]{:T(128)}) all-reduce(f32[]{:T(128)} %get-tuple-element.207, f32[]{:T(128)} %get-tuple-element.206), channel_id=1, replica_groups=mesh['gx'=8,'gy'=4] {'gy'}, use_global_device_ids=true, to_apply=%region_1.2 | all-reduce | flops 2 | bytes 16 | tf_op jit(solution)/shard_map/psum | solution.py:98
  125.1 20.1 %all-reduce.2 = (f32[]{:T(128)}, f32[]{:T(128)}) all-reduce(f32[]{:T(128)} %get-tuple-element.290, f32[]{:T(128)} %get-tuple-element.291), channel_id=1, replica_groups=mesh['gx'=8,'gy'=4] {'gx'}, use_global_device_ids=true, to_apply=%region_2.3 | all-reduce | flops 2 | bytes 16 | tf_op jit(solution)/shard_map/psum | solution.py:98
  148.7 1.9 collective-permute-done.9
  150.6 2.9 collective-permute-done.8
  154.1 2.3 collective-permute-done.11
  158.3 22.1 %while.37 = (s32[]{:T(128)}, f32[128,128]{1,0:T(8,128)S(1)}, f32[1152,128]{1,0:T(8,128)S(1)}, s32[]{:T(128)}, s32[384]{0:T(512)S(1)}, /*index=5*/f32[384,128]{1,...) while((s32[]{:T(128)}, f32[128,128]{1,0:T(8,128)S(1)}, ...), condition=%wide.region_18.19_spmd, body=%wide.region_15.18_spmd.sunk | while | flops 2140454 | bytes 2926959 | solution.py:93
  159.0 1.8 fusion.140
  180.5 2.0 collective-permute-start.12
  182.5 2.6 collective-permute-done.13
  185.1 63.5 %collective-permute-done.12 = bf16[3,128,128]{2,1,0:T(8,128)(2,1)S(1)} collective-permute-done((bf16[3,128,128]{2,1,0:T(8,128)(2,1)S(1)}, bf16[3,128,128]{2,1,0:T(8,128)(2,1)S(1)}, u32[]{:S(2)}, u32[]{:S(2)}) %collective-permute-start.12) | collective-permute-done | bytes 98336 | tf_op jit(solution)/shard_map/ppermute | solution.py:27
  252.8 6.3 %all-reduce.4 = (f32[]{:T(128)}, f32[]{:T(128)}) all-reduce(f32[]{:T(128)} %get-tuple-element.205, f32[]{:T(128)} %get-tuple-element.204), channel_id=1, replica_groups=mesh['gx'=8,'gy'=4] {'gy'}, use_global_device_ids=true, to_apply=%region_13.14 | all-reduce | flops 2 | bytes 16 | tf_op jit(solution)/shard_map/psum | solution.py:98
  259.2 19.8 %all-reduce.1 = (f32[]{:T(128)}, f32[]{:T(128)}) all-reduce(f32[]{:T(128)} %get-tuple-element.288, f32[]{:T(128)} %get-tuple-element.289), channel_id=1, replica_groups=mesh['gx'=8,'gy'=4] {'gx'}, use_global_device_ids=true, to_apply=%region_14.15 | all-reduce | flops 2 | bytes 16 | tf_op jit(solution)/shard_map/psum | solution.py:98
  283.5 2.0 collective-permute-start.16
  285.5 1.9 collective-permute-done.17
  287.4 2.8 collective-permute-done.16
  290.8 2.1 collective-permute-done.19
  292.8 2.2 collective-permute-done.18
  295.1 22.1 %while.38 = (s32[]{:T(128)}, f32[128,128]{1,0:T(8,128)S(1)}, f32[1152,128]{1,0:T(8,128)S(1)}, s32[]{:T(128)}, s32[384]{0:T(512)S(1)}, /*index=5*/f32[384,128]{1,...) while((s32[]{:T(128)}, f32[128,128]{1,0:T(8,128)S(1)}, ...), condition=%wide.region_28.29_spmd, body=%wide.region_25.28_spmd.sunk | while | flops 2140454 | bytes 2926959 | solution.py:93
  317.3 2.0 collective-permute-start.20
  319.4 2.6 collective-permute-done.21
  321.9 63.4 %collective-permute-done.20 = bf16[3,128,128]{2,1,0:T(8,128)(2,1)S(1)} collective-permute-done((bf16[3,128,128]{2,1,0:T(8,128)(2,1)S(1)}, bf16[3,128,128]{2,1,0:T(8,128)(2,1)S(1)}, u32[]{:S(2)}, u32[]{:S(2)}) %collective-permute-start.20) | collective-permute-done | bytes 98336 | tf_op jit(solution)/shard_map/ppermute | solution.py:27
  389.5 6.8 %all-reduce.3 = (f32[]{:T(128)}, f32[]{:T(128)}) all-reduce(f32[]{:T(128)} %get-tuple-element.203, f32[]{:T(128)} %get-tuple-element.202), channel_id=1, replica_groups=mesh['gx'=8,'gy'=4] {'gy'}, use_global_device_ids=true, to_apply=%region_23.24 | all-reduce | flops 2 | bytes 16 | tf_op jit(solution)/shard_map/psum | solution.py:98
  396.4 19.6 %all-reduce = (f32[]{:T(128)}, f32[]{:T(128)}) all-reduce(f32[]{:T(128)} %get-tuple-element.286, f32[]{:T(128)} %get-tuple-element.287), channel_id=1, replica_groups=mesh['gx'=8,'gy'=4] {'gx'}, use_global_device_ids=true, to_apply=%region_24.25 | all-reduce | flops 2 | bytes 16 | tf_op jit(solution)/shard_map/psum | solution.py:98
  (162 shorter events, 82.9 us)
Async XLA Ops:
  0.6 14.9 %copy-start.2 = (s32[128]{0:T(128)S(1)}, s32[128]{0:T(128)}, u32[]{:S(2)}) copy-start(s32[128]{0:T(128)} %param.15) | copy-start | bytes 1540
  0.6 14.9 %copy-start = (f32[128,128]{1,0:T(8,128)S(1)}, f32[128,128]{1,0:T(8,128)}, u32[]{:S(2)}) copy-start(f32[128,128]{1,0:T(8,128)} %param.13) | copy-start | bytes 196612
  0.7 15.8 %copy-start.3 = (s32[384]{0:T(512)S(1)}, s32[384]{0:T(512)}, u32[]{:S(2)}) copy-start(s32[384]{0:T(512)} %param.17) | copy-start | bytes 4612
  0.7 15.7 %copy-start.4 = (s32[384]{0:T(512)S(1)}, s32[384]{0:T(512)}, u32[]{:S(2)}) copy-start(s32[384]{0:T(512)} %param.16) | copy-start | bytes 4612
  1.6 14.0 %collective-permute-start.1 = (bf16[1,1,128,128]{3,2,1,0:T(8,128)(2,1)S(1)}, bf16[1,1,128,128]{3,2,1,0:T(8,128)(2,1)S(1)}, u32[]{:S(2)}, u32[]{:S(2)}) collective-permute-start(bf16[1,1,128,128]{3,2,1,0:T(8,128)(2,1)S(1)} %fusion.101), channel_id=1, source_target_pairs={{4,0},{8,4},{12,8},{16,12},{20,16},{24,20},{28,24},{0,28},{5,1},{9... | collective-permute-start | bytes 98312 | tf_op jit(solution)/shard_map/ppermute | solution.py:19
  7.7 7.9 %collective-permute-start = (bf16[1,1,128,128]{3,2,1,0:T(8,128)(2,1)S(1)}, bf16[1,1,128,128]{3,2,1,0:T(8,128)(2,1)S(1)}, u32[]{:S(2)}, u32[]{:S(2)}) collective-permute-start(bf16[1,1,128,128]{3,2,1,0:T(8,128)(2,1)S(1)} %fusion.101), channel_id=1, source_target_pairs={{0,4},{4,8},{8,12},{12,16},{16,20},{20,24},{24,28},{28,0},{1,5},{5... | collective-permute-start | bytes 98312 | tf_op jit(solution)/shard_map/ppermute | solution.py:16
  15.5 102.5 %copy-start.1 = (f32[128,128]{1,0:T(8,128)S(1)}, f32[128,128]{1,0:T(8,128)}, u32[]{:S(2)}) copy-start(f32[128,128]{1,0:T(8,128)} %param.14) | copy-start | bytes 196612
  15.7 3.6 collective-permute-start.3
  16.4 4.5 %collective-permute-start.2 = (bf16[3,1,128,128]{3,2,1,0:T(8,128)(2,1)S(1)}, bf16[3,1,128,128]{3,2,1,0:T(8,128)(2,1)S(1)}, u32[]{:S(2)}, u32[]{:S(2)}) collective-permute-start(bf16[3,1,128,128]{3,2,1,0:T(8,128)(2,1)S(1)} %pad_maximum_fusion.3), channel_id=1, source_target_pairs={{0,1},{1,2},{2,3},{3,0},{4,5},{5,6},{6,7},{7,4},{8,9},{9,10},{10,1... | collective-permute-start | bytes 294920 | tf_op jit(solution)/shard_map/ppermute | solution.py:16
  43.1 7.0 %collective-permute-start.5 = (bf16[3,128,128]{2,1,0:T(8,128)(2,1)S(1)}, bf16[3,128,128]{2,1,0:T(8,128)(2,1)S(1)}, u32[]{:S(2)}, u32[]{:S(2)}) collective-permute-start(bf16[3,128,128]{2,1,0:T(8,128)(2,1)S(1)} %bitcast.143), channel_id=1, source_target_pairs={{0,28},{4,0},{8,4},{12,8},{16,12},{20,16},{24,20},{28,24},{1,29},{... | collective-permute-start | bytes 294920 | tf_op jit(solution)/shard_map/ppermute | solution.py:27
  47.9 66.6 %collective-permute-start.4 = (bf16[3,128,128]{2,1,0:T(8,128)(2,1)S(1)}, bf16[3,128,128]{2,1,0:T(8,128)(2,1)S(1)}, u32[]{:S(2)}, u32[]{:S(2)}) collective-permute-start(bf16[3,128,128]{2,1,0:T(8,128)(2,1)S(1)} %bitcast.140), channel_id=1, source_target_pairs={{0,4},{4,8},{8,12},{12,16},{16,20},{20,24},{24,28},{28,0},{1,5},{5... | collective-permute-start | bytes 294920 | tf_op jit(solution)/shard_map/ppermute | solution.py:27
  114.6 1.7 collective-permute-start.7
  114.6 3.4 collective-permute-start.6
  146.6 4.0 collective-permute-start.9
  146.9 6.6 %collective-permute-start.8 = (bf16[1,1,128,128]{3,2,1,0:T(8,128)(2,1)S(1)}, bf16[1,1,128,128]{3,2,1,0:T(8,128)(2,1)S(1)}, u32[]{:S(2)}, u32[]{:S(2)}) collective-permute-start(bf16[1,1,128,128]{3,2,1,0:T(8,128)(2,1)S(1)} %bitcast.119), channel_id=1, source_target_pairs={{0,4},{4,8},{8,12},{12,16},{16,20},{20,24},{24,28},{28,0},{1,5},{5... | collective-permute-start | bytes 98312 | tf_op jit(solution)/shard_map/ppermute | solution.py:16
  153.5 2.9 collective-permute-start.11
  153.6 4.5 %collective-permute-start.10 = (bf16[3,1,128,128]{3,2,1,0:T(8,128)(2,1)S(1)}, bf16[3,1,128,128]{3,2,1,0:T(8,128)(2,1)S(1)}, u32[]{:S(2)}, u32[]{:S(2)}) collective-permute-start(bf16[3,1,128,128]{3,2,1,0:T(8,128)(2,1)S(1)} %pad_maximum_fusion.4), channel_id=1, source_target_pairs={{0,1},{1,2},{2,3},{3,0},{4,5},{5,6},{6,7},{7,4},{8,9},{9,10},{10,1... | collective-permute-start | bytes 294920 | tf_op jit(solution)/shard_map/ppermute | solution.py:16
  180.4 4.7 %collective-permute-start.13 = (bf16[3,128,128]{2,1,0:T(8,128)(2,1)S(1)}, bf16[3,128,128]{2,1,0:T(8,128)(2,1)S(1)}, u32[]{:S(2)}, u32[]{:S(2)}) collective-permute-start(bf16[3,128,128]{2,1,0:T(8,128)(2,1)S(1)} %bitcast.144), channel_id=1, source_target_pairs={{0,28},{4,0},{8,4},{12,8},{16,12},{20,16},{24,20},{28,24},{1,29},{... | collective-permute-start | bytes 294920 | tf_op jit(solution)/shard_map/ppermute | solution.py:27
  180.5 68.1 %collective-permute-start.12 = (bf16[3,128,128]{2,1,0:T(8,128)(2,1)S(1)}, bf16[3,128,128]{2,1,0:T(8,128)(2,1)S(1)}, u32[]{:S(2)}, u32[]{:S(2)}) collective-permute-start(bf16[3,128,128]{2,1,0:T(8,128)(2,1)S(1)} %bitcast.141), channel_id=1, source_target_pairs={{0,4},{4,8},{8,12},{12,16},{16,20},{20,24},{24,28},{28,0},{1,5},{5... | collective-permute-start | bytes 294920 | tf_op jit(solution)/shard_map/ppermute | solution.py:27
  248.7 1.7 collective-permute-start.15
  248.7 3.4 collective-permute-start.14
  283.5 4.0 collective-permute-start.17
  283.5 6.7 %collective-permute-start.16 = (bf16[1,1,128,128]{3,2,1,0:T(8,128)(2,1)S(1)}, bf16[1,1,128,128]{3,2,1,0:T(8,128)(2,1)S(1)}, u32[]{:S(2)}, u32[]{:S(2)}) collective-permute-start(bf16[1,1,128,128]{3,2,1,0:T(8,128)(2,1)S(1)} %bitcast.115), channel_id=1, source_target_pairs={{0,4},{4,8},{8,12},{12,16},{16,20},{20,24},{24,28},{28,0},{1,5},{5... | collective-permute-start | bytes 98312 | tf_op jit(solution)/shard_map/ppermute | solution.py:16
  290.2 2.6 collective-permute-start.19
  290.3 4.8 %collective-permute-start.18 = (bf16[3,1,128,128]{3,2,1,0:T(8,128)(2,1)S(1)}, bf16[3,1,128,128]{3,2,1,0:T(8,128)(2,1)S(1)}, u32[]{:S(2)}, u32[]{:S(2)}) collective-permute-start(bf16[3,1,128,128]{3,2,1,0:T(8,128)(2,1)S(1)} %pad_maximum_fusion.5), channel_id=1, source_target_pairs={{0,1},{1,2},{2,3},{3,0},{4,5},{5,6},{6,7},{7,4},{8,9},{9,10},{10,1... | collective-permute-start | bytes 294920 | tf_op jit(solution)/shard_map/ppermute | solution.py:16
  317.3 4.7 %collective-permute-start.21 = (bf16[3,128,128]{2,1,0:T(8,128)(2,1)S(1)}, bf16[3,128,128]{2,1,0:T(8,128)(2,1)S(1)}, u32[]{:S(2)}, u32[]{:S(2)}) collective-permute-start(bf16[3,128,128]{2,1,0:T(8,128)(2,1)S(1)} %bitcast.145), channel_id=1, source_target_pairs={{0,28},{4,0},{8,4},{12,8},{16,12},{20,16},{24,20},{28,24},{1,29},{... | collective-permute-start | bytes 294920 | tf_op jit(solution)/shard_map/ppermute | solution.py:27
  317.3 68.0 %collective-permute-start.20 = (bf16[3,128,128]{2,1,0:T(8,128)(2,1)S(1)}, bf16[3,128,128]{2,1,0:T(8,128)(2,1)S(1)}, u32[]{:S(2)}, u32[]{:S(2)}) collective-permute-start(bf16[3,128,128]{2,1,0:T(8,128)(2,1)S(1)} %bitcast.142), channel_id=1, source_target_pairs={{0,4},{4,8},{8,12},{12,16},{16,20},{20,24},{24,28},{28,0},{1,5},{5... | collective-permute-start | bytes 294920 | tf_op jit(solution)/shard_map/ppermute | solution.py:27
  385.4 1.7 collective-permute-start.23
  385.4 3.4 collective-permute-start.22
